TPU v7x, 256 devices: a whole 4x4x8 slice. The times are simulated.
256 devices in a mesh: batch: 4 (over z_lo, core), row: 4 (over x), col: 16 (over y, z_hi).
Axes of the slice: x: 4, y: 4, z: 8 (z_hi: 4, z_lo: 2; z = z_hi * 2 + z_lo), core: 2. Of those that a mesh axis runs over, the one named last changes fastest.
Arguments:
- embeddings: bfloat16 [512, 128, 512], P('batch', 'col', 'row'), may hold values from -170 to 170
- projection: bfloat16 [512, 32], replicated, may hold values from -0.25 to 0.25
- w_in: bfloat16 [16384, 2048], P('row', 'col'), may hold values from -0.046875 to 0.046875
- bias: float32 [2048], P('col'), may hold values from -3 to 3
- w_out: bfloat16 [2048, 128, 512], P(None, 'col', 'row'), may hold values from -0.125 to 0.125
- cotangent: bfloat16 [512, 128, 512], P('batch', 'col', 'row'), may hold values from -0.1796875 to 0.1796875
Outputs:
- mixed: bfloat16 [512, 128, 512], P('batch', 'col', 'row')
- grad_out: float32 [2048, 128, 512], P('batch', 'col', 'row')
- grad_in: float32 [16384, 2048], P('row', 'col')
- grad_bias: float32 [2048], P('col')
- grad_proj: float32 [512, 32], P('row')
All inputs are finite; a program needn't handle non-finite values.
Results may differ from a plain program's by a relative error of at most 0.006.
Values may be sent and summed in bfloat16 or wider, within the bound.
A program may use at most 128 MiB of HBM per device.

v0:
```python
import jax
import jax.numpy as jnp
from jax import lax
from jax.sharding import PartitionSpec as P

epsilon = 1e-06


def copy_for_each(array, axis):
    size = lax.axis_size(axis)
    return lax.all_to_all(
        jnp.broadcast_to(array[None], (size, *array.shape)), axis, 0, 0, tiled=True
    )


def of_everyone(array, axis):
    everything = copy_for_each(array, axis)
    return jnp.sum(everything, axis=0)


def joined_along(tiles, dim):
    tiles = jnp.moveaxis(tiles, 0, dim)
    lengths = tiles.shape
    return tiles.reshape(*lengths[:dim], lengths[dim] * lengths[dim + 1], *lengths[dim + 2 :])


def gathered_copies(array, axis, dim):
    return joined_along(copy_for_each(array, axis), dim)


def cut_along(array, dim, size):
    lengths = array.shape
    tiles = array.reshape(*lengths[:dim], size, lengths[dim] // size, *lengths[dim + 1 :])
    return jnp.moveaxis(tiles, dim, 0)


def sent_and_summed(array, axis, dim):
    size = lax.axis_size(axis)
    tiles = lax.all_to_all(cut_along(array, dim, size), axis, 0, 0, tiled=True)
    return jnp.sum(tiles, axis=0)


def in_one_piece(arrays, axis, dim, along):
    both = jnp.concatenate(arrays, axis=along)
    whole, at, gathered = (lax.all_gather(both, axis, axis=dim, tiled=True), 0, [])
    for a in arrays:
        gathered.append(lax.slice_in_dim(whole, at, at + a.shape[along], axis=along))
        at += a.shape[along]
    return tuple(gathered)


def filled_up(lines, size):
    spare = -lines.shape[0] % size
    if not spare:
        return lines
    return jnp.concatenate([lines, jnp.zeros((spare, *lines.shape[1:]), lines.dtype)])


def sum_by_parts(array, axis):
    lines = array.reshape(-1, *array.shape[1:][-1:])
    padded = filled_up(lines, lax.axis_size(axis))
    own = lax.psum_scatter(padded, axis, scatter_dimension=0, tiled=True)
    whole = lax.all_gather(own, axis, axis=0, tiled=True)
    return whole[: len(lines)].reshape(array.shape)


def contract_first(left, right):
    return lax.dot_general(
        left, right, (((0,), (0,)), ((), ())), preferred_element_type=jnp.float32
    )


def contract_last(left, right):
    return lax.dot_general(
        left, right, (((1,), (1,)), ((), ())), preferred_element_type=jnp.float32
    )


def local(embeddings, projection, w_in, bias, w_out, cotangent):
    highest = lax.Precision.HIGHEST
    tok_rows, feat_local, emb_local = embeddings.shape
    rank_cols = projection.shape[1]
    row_count = lax.axis_size("row")
    row_place = lax.axis_index("row")
    emb_float = embeddings.astype(jnp.float32)
    own_proj = lax.dynamic_slice_in_dim(projection, row_place * emb_local, emb_local, 0)
    folded = of_everyone(
        jnp.einsum("bde,ek->bdk", embeddings, own_proj, preferred_element_type=jnp.float32), "row"
    )
    partial_value = jnp.einsum("bde,bdk->bek", emb_float, folded, precision=highest)
    interact = lax.psum(partial_value, "col")
    feature_count = emb_local * row_count * rank_cols
    square_sum = of_everyone(jnp.sum(interact * interact, axis=(1, 2)), "row")
    inv_rms = lax.rsqrt(square_sum / feature_count + epsilon)[:, None, None]
    normed = interact * inv_rms
    activated = normed.astype(jnp.bfloat16).reshape(tok_rows, emb_local * rank_cols)
    preact = of_everyone(jnp.dot(activated, w_in, preferred_element_type=jnp.float32), "row") + bias
    hidden = jax.nn.silu(preact).astype(jnp.bfloat16)
    hidden_all = gathered_copies(hidden, "col", 1)
    flat_out = w_out.reshape(w_out.shape[0], feat_local * emb_local)
    mixed = (
        jnp.dot(hidden_all, flat_out, preferred_element_type=jnp.float32)
        .astype(jnp.bfloat16)
        .reshape(tok_rows, feat_local, emb_local)
    )
    cot_rows = cotangent.reshape(tok_rows, feat_local * emb_local)
    d_cols = sent_and_summed(contract_last(cot_rows, flat_out), "col", 1)
    d_hidden = of_everyone(d_cols, "row")
    sigmoid_pre = jax.nn.sigmoid(preact)
    d_preact = d_hidden * sigmoid_pre * (1.0 + preact * (1.0 - sigmoid_pre))
    d_pre_b = d_preact.astype(jnp.bfloat16)
    per_batch = w_out.shape[0] // lax.axis_size("batch")
    every_hidden, every_cot = in_one_piece((hidden_all, cot_rows), "batch", 0, 1)
    own_hidden = lax.dynamic_slice_in_dim(
        every_hidden, lax.axis_index("batch") * per_batch, per_batch, 1
    )
    grad_flat = contract_first(own_hidden, every_cot)
    grad_out = grad_flat.reshape(per_batch, feat_local, emb_local)
    grad_in, grad_bias = lax.psum(
        (contract_first(activated, d_pre_b), jnp.sum(d_preact, axis=0)), "batch"
    )
    d_act = sum_by_parts(contract_last(d_pre_b, w_in), "col").reshape(
        tok_rows, emb_local, rank_cols
    )
    inner_term = of_everyone(jnp.sum(d_act * normed, axis=(1, 2)), "row") / feature_count
    d_inter = (inv_rms * (d_act - normed * inner_term[:, None, None])).astype(jnp.bfloat16)
    back_fold = of_everyone(
        jnp.einsum("bek,bde->bdk", d_inter, embeddings, preferred_element_type=jnp.float32), "row"
    )
    grad_proj = of_everyone(
        jnp.einsum("bde,bdk->ek", emb_float, back_fold, precision=highest), ("batch", "col")
    )
    return (mixed, grad_out, grad_in, grad_bias, grad_proj)


def solution(mesh):
    placed = (
        P("batch", "col", "row"),
        P(),
        P("row", "col"),
        P("col"),
        P(None, "col", "row"),
        P("batch", "col", "row"),
    )
    return jax.shard_map(
        local,
        mesh=mesh,
        in_specs=placed,
        out_specs=(
            P("batch", "col", "row"),
            P("batch", "col", "row"),
            P("row", "col"),
            P("col"),
            P("row", None),
        ),
        check_vma=False,
    )
```

profile of v0, /device:TPU:1, one launch (start us, length us, event | category | flops | bytes accessed | tf_op | source)
XLA Modules:
  0.0 535.5 jit_solution(8240638500809765838)
XLA Ops:
  9.3 4.8 all-to-all-start
  14.4 7.4 %dot_general.47 = bf16[16,128,1024]{2,1,0:T(8,128)(2,1)} reshape(bf16[2048,8,128]{2,1,0:T(8,128)(2,1)} %param.10) | data formatting | bytes 8388608 | tf_op jit(solution)/shard_map/dot_general | solution.py:74
  22.1 3.2 convolution_bitcast_fusion.1
  25.3 4.7 convolution_bitcast_fusion.2
  30.0 11.6 %all-to-all-start.4 = ((f32[16,128,128]{2,1,0:T(8,128)}), f32[16,128,128]{2,1,0:T(8,128)}, u32[]{:S(2)}, u32[]{:S(2)}) async-start(f32[16,128,128]{2,1,0:T(8,128)} %convolution_bitcast_fusion.2), calls=%async_computation.4 | async-start | bytes 2097152 | tf_op jit(solution)/shard_map/all_to_all | solution.py:39
  41.6 172.1 %all-reduce.3.cloned.1.call-done = f32[128,128,32]{1,2,0:T(8,128)} async-done(((f32[128,128,32]{1,2,0:T(8,128)}), f32[128,128,32]{1,2,0:T(8,128)}) %all-reduce.3.cloned.1.call-update) | async-done | bytes 2097168 | tf_op jit(solution)/shard_map/psum | solution.py:91
  217.0 3.3 all-to-all-start.1
  225.1 4.0 all-to-all-start.5
  230.4 3.3 copy.58
  236.1 4.2 all-to-all-start.2
  241.3 5.8 %all-to-all-done.2 = f32[4,128,128]{2,1,0:T(8,128)} async-done(((f32[4,128,128]{2,1,0:T(8,128)}), f32[4,128,128]{2,1,0:T(8,128)}, u32[]{:S(2)}, u32[]{:S(2)}) %all-to-all-start.2) | async-done | bytes 262176 | tf_op jit(solution)/shard_map/all_to_all | solution.py:11
  251.4 95.4 %reduce-scatter.2.cloned.1.call-done = f32[8,4096]{1,0:T(8,128)} async-done(((f32[128,4096]{1,0:T(8,128)}), f32[8,4096]{1,0:T(8,128)}) %reduce-scatter.2.cloned.1.call-update) | async-done | bytes 131088 | tf_op jit(solution)/shard_map/reduce_scatter | solution.py:62
  347.1 23.1 %all_to_all.47 = bf16[16,128,128]{1,2,0:T(8,128)(2,1)S(1)} all-to-all(bf16[16,128,128]{1,2,0:T(8,128)(2,1)S(1)} %broadcast_in_dim.19), channel_id=1, replica_groups=mesh['batch'=4,'row'=4,'col'=16] {'col'}, dimensions={0} | all-to-all | bytes 1048576 | tf_op jit(solution)/shard_map/all_to_all | solution.py:11
  372.9 34.7 %all-gather.5.cloned.1.call-done = f32[128,4096]{1,0:T(8,128)} async-done(((f32[8,4096]{1,0:T(8,128)}), f32[128,4096]{1,0:T(8,128)}) %all-gather.5.cloned.1.call-update) | async-done | bytes 2097168 | tf_op jit(solution)/shard_map/all_gather | solution.py:63
  410.5 3.4 copy.65
  413.9 3.5 multiply_reduce_fusion
  417.3 8.2 %all_to_all.48 = f32[4,1,128]{2,1,0:T(1,128)S(1)} all-to-all(f32[4,1,128]{2,1,0:T(1,128)S(1)} %broadcast_in_dim.21), channel_id=1, replica_groups=mesh['batch'=4,'row'=4,'col'=16] {'row'}, dimensions={0} | all-to-all | bytes 4096 | tf_op jit(solution)/shard_map/all_to_all | solution.py:11
  425.5 3.1 convolution_bitcast_fusion.3
  430.8 3.5 all-to-all-start.7
  436.2 5.1 all-to-all-done.7
  442.6 10.9 %all-to-all-start.8 = ((f32[64,128,32]{1,2,0:T(8,128)}), f32[64,128,32]{1,2,0:T(8,128)S(1)}, u32[]{:S(2)}, u32[]{:S(2)}) async-start(f32[64,128,32]{1,2,0:T(8,128)} %broadcast_in_dim.23), calls=%async_computation.9 | async-start | bytes 2097152 | tf_op jit(solution)/shard_map/all_to_all | solution.py:11
  453.6 33.7 %psum.23 = f32[128]{0:T(128)} all-reduce(f32[128]{0:T(128)S(1)} %get-tuple-element.5), channel_id=1, replica_groups=mesh['batch'=4,'row'=4,'col'=16] {'batch'}, use_global_device_ids=true, to_apply=%region_9.10 | all-reduce | flops 128 | bytes 1024 | tf_op jit(solution)/shard_map/psum | solution.py:119
  497.1 28.8 %all-reduce.5.cloned.1.call-done = f32[4096,128]{1,0:T(8,128)} async-done(((f32[4096,128]{1,0:T(8,128)}), f32[4096,128]{1,0:T(8,128)}) %all-reduce.5.cloned.1.call-update) | async-done | bytes 2097168 | tf_op jit(solution)/shard_map/psum | solution.py:119
  525.9 3.0 copy.87
  (72 shorter events, 40.8 us)
Async XLA Ops:
  7.2 226.5 %copy-start = (bf16[4096,128]{1,0:T(8,128)(2,1)S(1)}, bf16[4096,128]{1,0:T(8,128)(2,1)}, u32[]{:S(2)}) copy-start(bf16[4096,128]{1,0:T(8,128)(2,1)} %param.8) | copy-start | bytes 3145732
  7.2 7.0 %copy-start.7 = (bf16[128,8,128]{2,1,0:T(8,128)(2,1)S(1)}, bf16[128,8,128]{2,1,0:T(8,128)(2,1)}, u32[]{:S(2)}) copy-start(bf16[128,8,128]{2,1,0:T(8,128)(2,1)} %param.11) | copy-start | bytes 786436
  9.3 12.5 %all-to-all-start = ((f32[4,128,8,32]{1,3,2,0:T(8,128)}), f32[4,128,8,32]{1,3,2,0:T(8,128)S(1)}, u32[]{:S(2)}, u32[]{:S(2)}) async-start(f32[4,128,8,32]{1,3,2,0:T(8,128)} %broadcast_in_dim.16), calls=%async_computation | async-start | bytes 1048576 | tf_op jit(solution)/shard_map/all_to_all | solution.py:11
  14.2 199.5 %all-reduce.3.cloned.1.call-start = ((), (), s32[]{:S(2)}) async-start(), calls=%async_computation.10 | async-start | bytes 4194304 | tf_op jit(solution)/shard_map/psum | solution.py:91
  14.4 10.9 %copy-start.4 = (bf16[128,8,128]{0,2,1:T(8,128)(2,1)}, bf16[128,8,128]{0,2,1:T(8,128)(2,1)S(1)}, u32[]{:S(2)}) copy-start(bf16[128,8,128]{0,2,1:T(8,128)(2,1)S(1)} %copy.60) | copy-start | bytes 786436
  14.4 7.7 %copy-start.3 = (bf16[128,8,128]{2,1,0:T(8,128)(2,1)S(1)}, bf16[128,8,128]{2,1,0:T(8,128)(2,1)}, u32[]{:S(2)}) copy-start(bf16[128,8,128]{2,1,0:T(8,128)(2,1)} %param.6) | copy-start | bytes 786436
  30.0 186.4 %all-to-all-start.4 = ((f32[16,128,128]{2,1,0:T(8,128)}), f32[16,128,128]{2,1,0:T(8,128)}, u32[]{:S(2)}, u32[]{:S(2)}) async-start(f32[16,128,128]{2,1,0:T(8,128)} %convolution_bitcast_fusion.2), calls=%async_computation.4 | async-start | bytes 2097152 | tf_op jit(solution)/shard_map/all_to_all | solution.py:39
  213.7 15.5 %copy-start.1 = (f32[128,128,32]{1,2,0:T(8,128)S(1)}, f32[128,128,32]{1,2,0:T(8,128)}, u32[]{:S(2)}) copy-start(f32[128,128,32]{1,2,0:T(8,128)} %all-reduce.3.cloned.1.call-done) | copy-start | bytes 6291460
  217.0 7.4 %all-to-all-start.1 = ((f32[4,1,128]{2,1,0:T(1,128)}), f32[4,1,128]{2,1,0:T(1,128)S(1)}, u32[]{:S(2)}, u32[]{:S(2)}) async-start(f32[4,1,128]{2,1,0:T(1,128)} %broadcast_in_dim.17), calls=%async_computation.1 | async-start | bytes 4096 | tf_op jit(solution)/shard_map/all_to_all | solution.py:11
  225.1 10.3 %all-to-all-start.5 = ((f32[4,128,128]{2,1,0:T(8,128)}), f32[4,128,128]{2,1,0:T(8,128)}, u32[]{:S(2)}, u32[]{:S(2)}) async-start(f32[4,128,128]{2,1,0:T(8,128)} %broadcast_in_dim.20), calls=%async_computation.5 | async-start | bytes 524288 | tf_op jit(solution)/shard_map/all_to_all | solution.py:11
  233.7 15.0 %copy-start.8 = (f32[128]{0:T(128)S(1)}, f32[128]{0:T(128)}, u32[]{:S(2)}) copy-start(f32[128]{0:T(128)} %param.9) | copy-start | bytes 1540
  236.1 10.9 %all-to-all-start.2 = ((f32[4,128,128]{2,1,0:T(8,128)}), f32[4,128,128]{2,1,0:T(8,128)}, u32[]{:S(2)}, u32[]{:S(2)}) async-start(f32[4,128,128]{2,1,0:T(8,128)} %broadcast_in_dim.18), calls=%async_computation.2 | async-start | bytes 524288 | tf_op jit(solution)/shard_map/all_to_all | solution.py:11
  240.3 106.5 %reduce-scatter.2.cloned.1.call-start = ((), (), s32[]{:S(2)}) async-start(), calls=%async_computation.13 | async-start | bytes 2228224 | tf_op jit(solution)/shard_map/reduce_scatter | solution.py:62
  251.4 156.3 %all-gather.5.cloned.1.call-start = ((), (), s32[]{:S(2)}) async-start(), calls=%async_computation.14 | async-start | bytes 2228224 | tf_op jit(solution)/shard_map/all_gather | solution.py:63
  346.9 144.2 %all-gather.3.cloned.1.call-start = ((), (), s32[]{:S(2)}) async-start(), calls=%async_computation.11 | async-start | bytes 3932160 | tf_op jit(solution)/shard_map/all_gather | solution.py:45
  370.2 0.8 copy-start.5
  428.7 5.7 %copy-start.2 = (bf16[128,128,32]{0,2,1:T(8,128)(2,1)S(1)}, bf16[128,128,32]{0,2,1:T(8,128)(2,1)}, u32[]{:S(2)}) copy-start(bf16[128,128,32]{0,2,1:T(8,128)(2,1)} %copy.58) | copy-start | bytes 3145732
  430.8 10.4 %all-to-all-start.7 = ((f32[4,128,8,32]{1,3,2,0:T(8,128)}), f32[4,128,8,32]{1,3,2,0:T(8,128)S(1)}, u32[]{:S(2)}, u32[]{:S(2)}) async-start(f32[4,128,8,32]{1,3,2,0:T(8,128)} %broadcast_in_dim.22), calls=%async_computation.8 | async-start | bytes 1048576 | tf_op jit(solution)/shard_map/all_to_all | solution.py:11
  434.3 91.6 %all-reduce.5.cloned.1.call-start = ((), (), s32[]{:S(2)}) async-start(), calls=%async_computation.12 | async-start | bytes 4194304 | tf_op jit(solution)/shard_map/psum | solution.py:119
  436.1 51.2 %copy-start.6 = (bf16[16,128,128]{1,2,0:T(8,128)(2,1)S(1)}, bf16[16,128,128]{1,2,0:T(8,128)(2,1)}, u32[]{:S(2)}) copy-start(bf16[16,128,128]{1,2,0:T(8,128)(2,1)} %copy-done.5) | copy-start | bytes 1572868
  442.6 53.8 %all-to-all-start.8 = ((f32[64,128,32]{1,2,0:T(8,128)}), f32[64,128,32]{1,2,0:T(8,128)S(1)}, u32[]{:S(2)}, u32[]{:S(2)}) async-start(f32[64,128,32]{1,2,0:T(8,128)} %broadcast_in_dim.23), calls=%async_computation.9 | async-start | bytes 2097152 | tf_op jit(solution)/shard_map/all_to_all | solution.py:11
  491.1 1.6 slice-start
Sparse Core Ops, SparseCore 0:
  25.4 188.1 all-reduce.2
  251.5 95.3 reduce-scatter.1
  349.3 58.3 all-gather.4
  409.3 39.9 all-gather.2
  452.4 73.5 all-reduce.4
where the time goes:
time: 537 us; the launch traced here: 536 us
  waiting for transfers between devices  345 us (64%)
  blocking collectives  65 us (12%)
  starting transfers between devices  42.5 us (8%)
  local copies, waits for them, and re-layouts  31.8 us (6%)
  matrix products  22.6 us (4%)
  other arithmetic  14.9 us (3%)
  between operations  14 us (3%)
    psum x1, waiting for transfers between devices, local(): interact = lax.psum(partial_value, 'col')  172 us
    reduce_scatter x1, waiting for transfers between devices, sum_by_parts(): own = lax.psum_scatter(padded, axis, scatter_dimension=0, tiled=True)  95.4 us
    all_gather x1, waiting for transfers between devices, sum_by_parts(): whole = lax.all_gather(own, axis, axis=0, tiled=True)  34.7 us
    psum x1, blocking collectives, local(): lax.psum((contract_first(activated, d_pre_b), jnp.sum(d_preact, axis=0)),...  33.7 us
    all_to_all x2, blocking collectives, copy_for_each(): lax.all_to_all(jnp.broadcast_to(array[None], (size, *array.shape)), axis,...  31.3 us
    all_to_all x6, starting transfers between devices, copy_for_each(): lax.all_to_all(jnp.broadcast_to(array[None], (size, *array.shape)), axis,...  30.8 us
    psum x1, waiting for transfers between devices, local(): lax.psum((contract_first(activated, d_pre_b), jnp.sum(d_preact, axis=0)),...  28.8 us
    all_to_all x6, waiting for transfers between devices, copy_for_each(): lax.all_to_all(jnp.broadcast_to(array[None], (size, *array.shape)), axis,...  13.6 us
  transfers between devices with their start and end apart: 12, of which 7 were waited for; matrix products, arithmetic and copies ran while one was open for 10% of the time, Pallas kernels for 0%

commit v1 on v0

--- a/solution.py
+++ b/solution.py
@@ -60,7 +60,9 @@
     lines = array.reshape(-1, *array.shape[1:][-1:])
     padded = filled_up(lines, lax.axis_size(axis))
     own = lax.psum_scatter(padded, axis, scatter_dimension=0, tiled=True)
-    whole = lax.all_gather(own, axis, axis=0, tiled=True)
+    whole = jnp.concatenate(
+        lax.all_to_all(jnp.stack([own] * lax.axis_size(axis)), axis, 0, 0), axis=0
+    )
     return whole[: len(lines)].reshape(array.shape)
 
 

time: 537 us -> 555 us (1.034)
  starting transfers between devices: 42.5 us -> 54.6 us
  local copies, waits for them, and re-layouts: 31.8 us -> 39.7 us
    all_to_all x0 -> x1, waiting for transfers between devices: none -> 56.9 us  [sum_by_parts(): lax.all_to_all(jnp.stack([own] * lax.axis_size(axis)), axis, 0, 0)]
    all_gather x1 -> x0, waiting for transfers between devices: 34.7 us -> none  [sum_by_parts(): whole = lax.all_gather(own, axis, axis=0, tiled=True)]
    reduce_scatter x1, waiting for transfers between devices: 95.4 us -> 79.8 us  [sum_by_parts(): own = lax.psum_scatter(padded, axis, scatter_dimension=0, tiled=True)]
    another operation x0 -> x3, local copies, waits for them, and re-layouts: none -> 15.1 us  [the longest x2 12.7 us: local(): sum_by_parts(contract_last(d_pre_b, w_in), 'col')]
    psum x1, waiting for transfers between devices: 28.8 us -> 21.5 us  [local(): lax.psum((contract_first(activated, d_pre_b), jnp.sum(d_preact, axis=0)),...]
    all_to_all x6, starting transfers between devices: 30.8 us -> 36.8 us  [copy_for_each(): lax.all_to_all(jnp.broadcast_to(array[None], (size, *array.shape)), axis,...]
    all_to_all x0 -> x1, starting transfers between devices: none -> 5.92 us  [sum_by_parts(): lax.all_to_all(jnp.stack([own] * lax.axis_size(axis)), axis, 0, 0)]
    all_to_all x2, blocking collectives: 31.3 us -> 25.7 us  [copy_for_each(): lax.all_to_all(jnp.broadcast_to(array[None], (size, *array.shape)), axis,...]
  transfers between devices with their start and end apart: 12 -> 12, of which waited for: 7 -> 7; matrix products, arithmetic and copies ran while one was open for 10% -> 11% of each run, Pallas kernels for 0% -> 0%
where the time goes in v1:
time: 555 us; the launch traced here: 554 us
  waiting for transfers between devices  344 us (62%)
  blocking collectives  63.9 us (12%)
  starting transfers between devices  54.6 us (10%)
  local copies, waits for them, and re-layouts  39.7 us (7%)
  matrix products  22.5 us (4%)
  other arithmetic  15.1 us (3%)
  between operations  14 us (3%)
    psum x1, waiting for transfers between devices, local(): interact = lax.psum(partial_value, 'col')  172 us
    reduce_scatter x1, waiting for transfers between devices, sum_by_parts(): own = lax.psum_scatter(padded, axis, scatter_dimension=0, tiled=True)  79.8 us
    all_to_all x1, waiting for transfers between devices, sum_by_parts(): lax.all_to_all(jnp.stack([own] * lax.axis_size(axis)), axis, 0, 0)  56.9 us
    psum x1, blocking collectives, local(): lax.psum((contract_first(activated, d_pre_b), jnp.sum(d_preact, axis=0)),...  38.3 us
    all_to_all x6, starting transfers between devices, copy_for_each(): lax.all_to_all(jnp.broadcast_to(array[None], (size, *array.shape)), axis,...  36.8 us
    all_to_all x2, blocking collectives, copy_for_each(): lax.all_to_all(jnp.broadcast_to(array[None], (size, *array.shape)), axis,...  25.7 us
    psum x1, waiting for transfers between devices, local(): lax.psum((contract_first(activated, d_pre_b), jnp.sum(d_preact, axis=0)),...  21.5 us
    all_to_all x6, waiting for transfers between devices, copy_for_each(): lax.all_to_all(jnp.broadcast_to(array[None], (size, *array.shape)), axis,...  13.4 us
  transfers between devices with their start and end apart: 12, of which 7 were waited for; matrix products, arithmetic and copies ran while one was open for 11% of the time, Pallas kernels for 0%

profile of v1, /device:TPU:1, one launch (start us, length us, event | category | flops | bytes accessed | tf_op | source)
XLA Modules:
  0.0 553.5 jit_solution(11179634422010670983)
XLA Ops:
  9.3 4.8 all-to-all-start
  14.4 7.4 %dot_general.47 = bf16[16,128,1024]{2,1,0:T(8,128)(2,1)} reshape(bf16[2048,8,128]{2,1,0:T(8,128)(2,1)} %param.10) | data formatting | bytes 8388608 | tf_op jit(solution)/shard_map/dot_general | solution.py:76
  22.1 3.2 convolution_bitcast_fusion.1
  25.3 4.7 convolution_bitcast_fusion.2
  30.0 11.6 %all-to-all-start.4 = ((f32[16,128,128]{2,1,0:T(8,128)}), f32[16,128,128]{2,1,0:T(8,128)}, u32[]{:S(2)}, u32[]{:S(2)}) async-start(f32[16,128,128]{2,1,0:T(8,128)} %convolution_bitcast_fusion.2), calls=%async_computation.4 | async-start | bytes 2097152 | tf_op jit(solution)/shard_map/all_to_all | solution.py:39
  41.6 172.1 %all-reduce.3.cloned.1.call-done = f32[128,128,32]{1,2,0:T(8,128)} async-done(((f32[128,128,32]{1,2,0:T(8,128)}), f32[128,128,32]{1,2,0:T(8,128)}) %all-reduce.3.cloned.1.call-update) | async-done | bytes 2097168 | tf_op jit(solution)/shard_map/psum | solution.py:93
  217.0 3.3 all-to-all-start.1
  225.1 4.0 all-to-all-start.5
  230.4 3.2 copy.54
  236.0 4.2 all-to-all-start.2
  241.2 5.7 %all-to-all-done.2 = f32[4,128,128]{2,1,0:T(8,128)} async-done(((f32[4,128,128]{2,1,0:T(8,128)}), f32[4,128,128]{2,1,0:T(8,128)}, u32[]{:S(2)}, u32[]{:S(2)}) %all-to-all-start.2) | async-done | bytes 262176 | tf_op jit(solution)/shard_map/all_to_all | solution.py:11
  251.4 17.9 %all_to_all.52 = bf16[16,128,128]{1,2,0:T(8,128)(2,1)} all-to-all(bf16[16,128,128]{1,2,0:T(8,128)(2,1)S(1)} %broadcast_in_dim.19), channel_id=1, replica_groups=mesh['batch'=4,'row'=4,'col'=16] {'col'}, dimensions={0} | all-to-all | bytes 1048576 | tf_op jit(solution)/shard_map/all_to_all | solution.py:11
  269.3 79.8 %reduce-scatter.2.cloned.1.call-done = f32[8,4096]{1,0:T(8,128)} async-done(((f32[128,4096]{1,0:T(8,128)}), f32[8,4096]{1,0:T(8,128)}) %reduce-scatter.2.cloned.1.call-update) | async-done | bytes 131088 | tf_op jit(solution)/shard_map/reduce_scatter | solution.py:62
  351.5 5.9 %all-to-all-start.6 = ((f32[16,8,4096]{2,1,0:T(8,128)}), f32[16,8,4096]{2,1,0:T(8,128)}, u32[]{:S(2)}, u32[]{:S(2)}) async-start(f32[16,8,4096]{2,1,0:T(8,128)} %stack.2), calls=%async_computation.7 | async-start | bytes 4194304 | tf_op jit(solution)/shard_map/all_to_all | solution.py:64
  359.5 56.9 %all-to-all-done.6 = f32[16,8,4096]{2,1,0:T(8,128)} async-done(((f32[16,8,4096]{2,1,0:T(8,128)}), f32[16,8,4096]{2,1,0:T(8,128)}, u32[]{:S(2)}, u32[]{:S(2)}) %all-to-all-start.6) | async-done | bytes 2097184 | tf_op jit(solution)/shard_map/all_to_all | solution.py:64
  416.4 6.4 %reshape_reshape.3 = f32[128,128,32]{2,1,0:T(8,128)} reshape(f32[16,8,4096]{2,1,0:T(8,128)} %all-to-all-done.6) | data formatting | bytes 4194304 | tf_op jit(solution)/shard_map/reshape;reshape | solution.py:124
  422.8 6.2 %copy.60 = f32[128,128,32]{1,2,0:T(8,128)} copy(f32[128,128,32]{2,1,0:T(8,128)} %reshape_reshape.3) | data formatting | bytes 4194304 | tf_op jit(solution)/shard_map/reshape;reshape | solution.py:124
  429.1 3.5 multiply_reduce_fusion
  432.6 7.8 %all_to_all.53 = f32[4,1,128]{2,1,0:T(1,128)S(1)} all-to-all(f32[4,1,128]{2,1,0:T(1,128)S(1)} %broadcast_in_dim.21), channel_id=1, replica_groups=mesh['batch'=4,'row'=4,'col'=16] {'row'}, dimensions={0} | all-to-all | bytes 4096 | tf_op jit(solution)/shard_map/all_to_all | solution.py:11
  445.6 3.5 all-to-all-start.8
  451.1 4.9 all-to-all-done.8
  457.4 17.0 %all-to-all-start.9 = ((f32[64,128,32]{1,2,0:T(8,128)}), f32[64,128,32]{1,2,0:T(8,128)S(1)}, u32[]{:S(2)}, u32[]{:S(2)}) async-start(f32[64,128,32]{1,2,0:T(8,128)} %broadcast_in_dim.23), calls=%async_computation.10 | async-start | bytes 2097152 | tf_op jit(solution)/shard_map/all_to_all | solution.py:11
  474.4 38.3 %psum.23 = f32[128]{0:T(128)} all-reduce(f32[128]{0:T(128)S(1)} %get-tuple-element.5), channel_id=1, replica_groups=mesh['batch'=4,'row'=4,'col'=16] {'batch'}, use_global_device_ids=true, to_apply=%region_9.10 | all-reduce | flops 128 | bytes 1024 | tf_op jit(solution)/shard_map/psum | solution.py:121
  522.4 21.5 %all-reduce.5.cloned.1.call-done = f32[4096,128]{1,0:T(8,128)} async-done(((f32[4096,128]{1,0:T(8,128)}), f32[4096,128]{1,0:T(8,128)}) %all-reduce.5.cloned.1.call-update) | async-done | bytes 2097168 | tf_op jit(solution)/shard_map/psum | solution.py:121
  (70 shorter events, 45.9 us)
Async XLA Ops:
  7.2 226.4 %copy-start = (bf16[4096,128]{1,0:T(8,128)(2,1)S(1)}, bf16[4096,128]{1,0:T(8,128)(2,1)}, u32[]{:S(2)}) copy-start(bf16[4096,128]{1,0:T(8,128)(2,1)} %param.8) | copy-start | bytes 3145732
  7.2 7.0 %copy-start.6 = (bf16[128,8,128]{2,1,0:T(8,128)(2,1)S(1)}, bf16[128,8,128]{2,1,0:T(8,128)(2,1)}, u32[]{:S(2)}) copy-start(bf16[128,8,128]{2,1,0:T(8,128)(2,1)} %param.11) | copy-start | bytes 786436
  9.3 12.5 %all-to-all-start = ((f32[4,128,8,32]{1,3,2,0:T(8,128)}), f32[4,128,8,32]{1,3,2,0:T(8,128)S(1)}, u32[]{:S(2)}, u32[]{:S(2)}) async-start(f32[4,128,8,32]{1,3,2,0:T(8,128)} %broadcast_in_dim.16), calls=%async_computation | async-start | bytes 1048576 | tf_op jit(solution)/shard_map/all_to_all | solution.py:11
  14.2 199.5 %all-reduce.3.cloned.1.call-start = ((), (), s32[]{:S(2)}) async-start(), calls=%async_computation.11 | async-start | bytes 4194304 | tf_op jit(solution)/shard_map/psum | solution.py:93
  14.4 10.9 %copy-start.4 = (bf16[128,8,128]{0,2,1:T(8,128)(2,1)}, bf16[128,8,128]{0,2,1:T(8,128)(2,1)S(1)}, u32[]{:S(2)}) copy-start(bf16[128,8,128]{0,2,1:T(8,128)(2,1)S(1)} %copy.56) | copy-start | bytes 786436
  14.4 7.7 %copy-start.3 = (bf16[128,8,128]{2,1,0:T(8,128)(2,1)S(1)}, bf16[128,8,128]{2,1,0:T(8,128)(2,1)}, u32[]{:S(2)}) copy-start(bf16[128,8,128]{2,1,0:T(8,128)(2,1)} %param.6) | copy-start | bytes 786436
  30.0 186.4 %all-to-all-start.4 = ((f32[16,128,128]{2,1,0:T(8,128)}), f32[16,128,128]{2,1,0:T(8,128)}, u32[]{:S(2)}, u32[]{:S(2)}) async-start(f32[16,128,128]{2,1,0:T(8,128)} %convolution_bitcast_fusion.2), calls=%async_computation.4 | async-start | bytes 2097152 | tf_op jit(solution)/shard_map/all_to_all | solution.py:39
  213.7 15.5 %copy-start.1 = (f32[128,128,32]{1,2,0:T(8,128)S(1)}, f32[128,128,32]{1,2,0:T(8,128)}, u32[]{:S(2)}) copy-start(f32[128,128,32]{1,2,0:T(8,128)} %all-reduce.3.cloned.1.call-done) | copy-start | bytes 6291460
  217.0 7.4 %all-to-all-start.1 = ((f32[4,1,128]{2,1,0:T(1,128)}), f32[4,1,128]{2,1,0:T(1,128)S(1)}, u32[]{:S(2)}, u32[]{:S(2)}) async-start(f32[4,1,128]{2,1,0:T(1,128)} %broadcast_in_dim.17), calls=%async_computation.1 | async-start | bytes 4096 | tf_op jit(solution)/shard_map/all_to_all | solution.py:11
  225.1 10.2 %all-to-all-start.5 = ((f32[4,128,128]{2,1,0:T(8,128)}), f32[4,128,128]{2,1,0:T(8,128)}, u32[]{:S(2)}, u32[]{:S(2)}) async-start(f32[4,128,128]{2,1,0:T(8,128)} %broadcast_in_dim.20), calls=%async_computation.5 | async-start | bytes 524288 | tf_op jit(solution)/shard_map/all_to_all | solution.py:11
  233.6 14.9 %copy-start.7 = (f32[128]{0:T(128)S(1)}, f32[128]{0:T(128)}, u32[]{:S(2)}) copy-start(f32[128]{0:T(128)} %param.9) | copy-start | bytes 1540
  236.0 10.9 %all-to-all-start.2 = ((f32[4,128,128]{2,1,0:T(8,128)}), f32[4,128,128]{2,1,0:T(8,128)}, u32[]{:S(2)}, u32[]{:S(2)}) async-start(f32[4,128,128]{2,1,0:T(8,128)} %broadcast_in_dim.18), calls=%async_computation.2 | async-start | bytes 524288 | tf_op jit(solution)/shard_map/all_to_all | solution.py:11
  240.2 108.8 %reduce-scatter.2.cloned.1.call-start = ((), (), s32[]{:S(2)}) async-start(), calls=%async_computation.14 | async-start | bytes 2228224 | tf_op jit(solution)/shard_map/reduce_scatter | solution.py:62
  351.5 65.0 %all-to-all-start.6 = ((f32[16,8,4096]{2,1,0:T(8,128)}), f32[16,8,4096]{2,1,0:T(8,128)}, u32[]{:S(2)}, u32[]{:S(2)}) async-start(f32[16,8,4096]{2,1,0:T(8,128)} %stack.2), calls=%async_computation.7 | async-start | bytes 4194304 | tf_op jit(solution)/shard_map/all_to_all | solution.py:64
  357.4 159.0 %all-gather.2.cloned.1.call-start = ((), (), s32[]{:S(2)}) async-start(), calls=%async_computation.12 | async-start | bytes 3932160 | tf_op jit(solution)/shard_map/all_gather | solution.py:45
  443.5 5.9 %copy-start.2 = (bf16[128,128,32]{0,2,1:T(8,128)(2,1)S(1)}, bf16[128,128,32]{0,2,1:T(8,128)(2,1)}, u32[]{:S(2)}) copy-start(bf16[128,128,32]{0,2,1:T(8,128)(2,1)} %copy.54) | copy-start | bytes 3145732
  445.6 10.4 %all-to-all-start.8 = ((f32[4,128,8,32]{1,3,2,0:T(8,128)}), f32[4,128,8,32]{1,3,2,0:T(8,128)S(1)}, u32[]{:S(2)}, u32[]{:S(2)}) async-start(f32[4,128,8,32]{1,3,2,0:T(8,128)} %broadcast_in_dim.22), calls=%async_computation.9 | async-start | bytes 1048576 | tf_op jit(solution)/shard_map/all_to_all | solution.py:11
  449.1 94.8 %all-reduce.5.cloned.1.call-start = ((), (), s32[]{:S(2)}) async-start(), calls=%async_computation.13 | async-start | bytes 4194304 | tf_op jit(solution)/shard_map/psum | solution.py:121
  451.1 61.6 %copy-start.5 = (bf16[16,128,128]{1,2,0:T(8,128)(2,1)S(1)}, bf16[16,128,128]{1,2,0:T(8,128)(2,1)}, u32[]{:S(2)}) copy-start(bf16[16,128,128]{1,2,0:T(8,128)(2,1)} %all_to_all.52) | copy-start | bytes 1572868
  457.4 64.3 %all-to-all-start.9 = ((f32[64,128,32]{1,2,0:T(8,128)}), f32[64,128,32]{1,2,0:T(8,128)S(1)}, u32[]{:S(2)}, u32[]{:S(2)}) async-start(f32[64,128,32]{1,2,0:T(8,128)} %broadcast_in_dim.23), calls=%async_computation.10 | async-start | bytes 2097152 | tf_op jit(solution)/shard_map/all_to_all | solution.py:11
  516.4 1.6 slice-start
Sparse Core Ops, SparseCore 0:
  25.4 188.1 all-reduce.2
  251.3 97.6 reduce-scatter.1
  360.0 69.1 all-gather.1
  452.9 91.0 all-reduce.4
